TPU v7x, 128 devices: a whole 4x4x4 slice. The times are simulated.
128 devices in a mesh: dp: 8 (over z_lo, y), pipe: 16 (over z_hi, x, core).
Axes of the slice: x: 4, y: 4, z: 4 (z_hi: 2, z_lo: 2; z = z_hi * 2 + z_lo), core: 2. Of those that a mesh axis runs over, the one named last changes fastest.
Arguments:
- activations: bfloat16 [16, 4096, 8192], P('pipe', 'dp'), may hold values from -6 to 6
- cotangent: bfloat16 [4096, 8192], P('dp'), may hold values from -6 to 6
- adapter_down: bfloat16 [16, 8192, 512], P('pipe'), may hold values from -0.0625 to 0.0625
- adapter_expand: bfloat16 [16, 512, 8192], P('pipe'), may hold values from -0.25 to 0.25
- value_rows: bfloat16 [16, 32, 8192], P('pipe', 'dp'), may hold values from -0.0625 to 0.0625
- input_rows: bfloat16 [16, 32, 8192], P('pipe', 'dp'), may hold values from -0.0625 to 0.0625
- hidden_cols: bfloat16 [16, 32, 512], P('pipe'), may hold values from -0.25 to 0.25
- inner_cols: bfloat16 [16, 32, 512], P('pipe'), may hold values from -0.25 to 0.25
- lengths: int32 [32], P('dp'), may hold values from 1 to 128, as said below
- query_example: int32 [32], replicated, may hold values from 0 to 31
Outputs:
- scores: float32 [32, 32], P('dp')
Inputs may be any that keep to these rules, and one draw needn't show every extreme that they name: `lengths`: live tokens of each example; the rest of its 128 positions is padding.
All inputs are finite; a program needn't handle non-finite values.
Results may differ from a plain program's by a relative error of at most 0.022.
Values may be sent and summed in bfloat16 or wider, within the bound.
A program may use at most 128 MiB of HBM per device.

v0:
```python
import jax
import jax.numpy as jnp
from jax import lax
from jax.sharding import PartitionSpec as P

SLOT = 128
adapter_scale = 0.25


def from_behind(value, axis, steps):
    count = lax.axis_size(axis)
    first, last = (max(0, -steps), min(count, count - steps))
    return lax.ppermute(value, axis, [(source, source + steps) for source in range(first, last)])


def local(
    activations,
    cotangent,
    adapter_down,
    adapter_expand,
    value_rows,
    input_rows,
    hidden_cols,
    inner_cols,
    lengths,
    query_example,
):
    section_total = lax.axis_size("pipe")
    section_index = lax.axis_index("pipe")
    tok_dev = activations.shape[1]
    ex_dev = tok_dev // SLOT
    query_total = hidden_cols.shape[1]
    value_all, input_all = (
        lax.all_gather(value_rows[0], "dp", axis=0, tiled=True),
        lax.all_gather(input_rows[0], "dp", axis=0, tiled=True),
    )
    down_map = adapter_down[0]
    up_map = adapter_expand[0]
    hid_factor = hidden_cols[0]
    inn_factor = inner_cols[0]
    act_local = activations[0]
    block_rows = SLOT
    block_count = tok_dev // block_rows
    step_count = block_count + section_total - 1
    is_last = section_index == section_total - 1

    def advance(step_index, carry):
        incoming, per_token = carry
        block_index = step_index - (section_total - 1 - section_index)
        is_valid = (block_index >= 0) & (block_index < block_count)
        row_start = jnp.clip(block_index, 0, block_count - 1) * block_rows
        seed_rows = lax.dynamic_slice_in_dim(cotangent, row_start, block_rows, 0)
        gradient_leaving = jnp.where(is_last, seed_rows, incoming)

        def compute(unused):
            act_rows = lax.dynamic_slice_in_dim(act_local, row_start, block_rows, 0)
            hidden = jnp.dot(act_rows, down_map, preferred_element_type=jnp.float32).astype(
                jnp.bfloat16
            )
            inner_gradient = (
                adapter_scale
                * jnp.einsum(
                    "td,rd->tr", gradient_leaving, up_map, preferred_element_type=jnp.float32
                )
            ).astype(jnp.bfloat16)
            gradient_entering = (
                gradient_leaving.astype(jnp.float32)
                + jnp.einsum(
                    "tr,dr->td", inner_gradient, down_map, preferred_element_type=jnp.float32
                )
            ).astype(jnp.bfloat16)
            hidden_projection = jnp.einsum(
                "tr,qr->tq", hidden, hid_factor, preferred_element_type=jnp.float32
            )
            value_projection = jnp.einsum(
                "td,qd->tq", gradient_leaving, value_all, preferred_element_type=jnp.float32
            )
            input_projection = jnp.einsum(
                "td,qd->tq", act_rows, input_all, preferred_element_type=jnp.float32
            )
            inner_projection = jnp.einsum(
                "tr,qr->tq", inner_gradient, inn_factor, preferred_element_type=jnp.float32
            )
            return (
                gradient_entering,
                adapter_scale * hidden_projection * value_projection
                + input_projection * inner_projection,
            )

        def skipped(unused):
            return (
                jnp.zeros_like(gradient_leaving),
                jnp.zeros((block_rows, query_total), jnp.float32),
            )

        gradient_entering, summand_rows = lax.cond(is_valid, compute, skipped, 0)
        previous = lax.dynamic_slice_in_dim(per_token, row_start, block_rows, 0)
        per_token = lax.dynamic_update_slice_in_dim(
            per_token, previous + summand_rows, row_start, 0
        )
        incoming = from_behind(gradient_entering, "pipe", -1)
        return (incoming, per_token)

    start_grad = jnp.zeros((block_rows, act_local.shape[1]), jnp.bfloat16)
    start_terms = jnp.zeros((tok_dev, query_total), jnp.float32)
    final_grad, per_token = lax.fori_loop(0, step_count, advance, (start_grad, start_terms))
    offsets = lax.broadcasted_iota(jnp.int32, (tok_dev,), 0) % SLOT
    live_mask = (offsets < jnp.repeat(lengths, SLOT, total_repeat_length=tok_dev)).astype(
        jnp.float32
    )
    masked = per_token * live_mask[:, None]
    local_sums = jnp.sum(masked.reshape(ex_dev, SLOT, query_total), axis=1)
    totals = lax.psum(local_sums, "pipe") * SLOT ** (-0.5)
    example_ids = lax.axis_index("dp") * ex_dev + lax.broadcasted_iota(jnp.int32, (ex_dev,), 0)
    keep_mask = (example_ids[:, None] != query_example[None, :]).astype(jnp.float32)
    return totals * keep_mask


def solution(mesh):
    in_specs = (
        P("pipe", "dp", None),
        P("dp", None),
        P("pipe", None, None),
        P("pipe", None, None),
        P("pipe", "dp", None),
        P("pipe", "dp", None),
        P("pipe", None, None),
        P("pipe", None, None),
        P("dp"),
        P(),
    )
    out_specs = P("dp", None)
    return jax.shard_map(local, mesh=mesh, in_specs=in_specs, out_specs=out_specs, check_vma=False)
```

profile of v0, /device:TPU:8, one launch (start us, length us, event | category | flops | bytes accessed | tf_op | source)
XLA Modules:
  0.0 913.3 jit_solution(10851682348993537943)
XLA Ops:
  1.0 31.1 %all-gather = bf16[1,32,8192]{2,0,1:T(2,128)(2,1)S(1)} all-gather(bf16[1,4,8192]{2,0,1:T(2,128)(2,1)S(1)} %copy.14), channel_id=2, replica_groups=mesh['dp'=8,'pipe'=16] {'dp'}, dimensions={1}, use_global_device_ids=true | all-gather | bytes 589824 | tf_op jit(solution)/shard_map/all_gather | solution.py:34
  32.7 30.5 %all-gather.1 = bf16[1,32,8192]{2,0,1:T(2,128)(2,1)S(1)} all-gather(bf16[1,4,8192]{2,0,1:T(2,128)(2,1)S(1)} %copy.15), channel_id=3, replica_groups=mesh['dp'=8,'pipe'=16] {'dp'}, dimensions={1}, use_global_device_ids=true | all-gather | bytes 589824 | tf_op jit(solution)/shard_map/all_gather | solution.py:35
  64.1 758.5 %while.18 = (s32[]{:T(128)}, bf16[128,8192]{1,0:T(8,128)(2,1)S(1)}, f32[512,32]{0,1:T(8,128)S(1)}, s32[]{:T(128)}, pred[]{:T(512)}, /*index=5*/bf16[512,8192]{1,...) while((s32[]{:T(128)}, bf16[128,8192]{1,0:T(8,128)(2,1)S(1)}, ...), condition=%wide.region_3.4_spmd, body=%wide.region_0.3_spmd.sunk | while | flops 3368243200 | bytes 79266320 | solution.py:106
  64.1 1.6 conditional.2
  64.2 1.5 broadcast.142
  67.0 4.9 collective-permute-done
  72.0 1.6 conditional.2
  74.8 25.6 %collective-permute-done = bf16[128,8192]{1,0:T(8,128)(2,1)S(1)} collective-permute-done((bf16[128,8192]{1,0:T(8,128)(2,1)}, bf16[128,8192]{1,0:T(8,128)(2,1)S(1)}, u32[]{:S(2)}, u32[]{:S(2)}) %collective-permute-start) | collective-permute-done | bytes 2097184 | tf_op jit(solution)/shard_map/while/body/eval_jaxpr/ppermute | solution.py:13
  100.4 1.6 conditional.2
  103.3 26.2 %collective-permute-done = bf16[128,8192]{1,0:T(8,128)(2,1)S(1)} collective-permute-done((bf16[128,8192]{1,0:T(8,128)(2,1)}, bf16[128,8192]{1,0:T(8,128)(2,1)S(1)}, u32[]{:S(2)}, u32[]{:S(2)}) %collective-permute-start) | collective-permute-done | bytes 2097184 | tf_op jit(solution)/shard_map/while/body/eval_jaxpr/ppermute | solution.py:13
  129.5 1.6 conditional.2
  132.4 26.2 %collective-permute-done = bf16[128,8192]{1,0:T(8,128)(2,1)S(1)} collective-permute-done((bf16[128,8192]{1,0:T(8,128)(2,1)}, bf16[128,8192]{1,0:T(8,128)(2,1)S(1)}, u32[]{:S(2)}, u32[]{:S(2)}) %collective-permute-start) | collective-permute-done | bytes 2097184 | tf_op jit(solution)/shard_map/while/body/eval_jaxpr/ppermute | solution.py:13
  158.6 1.6 conditional.2
  161.5 26.2 %collective-permute-done = bf16[128,8192]{1,0:T(8,128)(2,1)S(1)} collective-permute-done((bf16[128,8192]{1,0:T(8,128)(2,1)}, bf16[128,8192]{1,0:T(8,128)(2,1)S(1)}, u32[]{:S(2)}, u32[]{:S(2)}) %collective-permute-start) | collective-permute-done | bytes 2097184 | tf_op jit(solution)/shard_map/while/body/eval_jaxpr/ppermute | solution.py:13
  187.7 1.6 conditional.2
  190.6 26.2 %collective-permute-done = bf16[128,8192]{1,0:T(8,128)(2,1)S(1)} collective-permute-done((bf16[128,8192]{1,0:T(8,128)(2,1)}, bf16[128,8192]{1,0:T(8,128)(2,1)S(1)}, u32[]{:S(2)}, u32[]{:S(2)}) %collective-permute-start) | collective-permute-done | bytes 2097184 | tf_op jit(solution)/shard_map/while/body/eval_jaxpr/ppermute | solution.py:13
  216.9 1.6 conditional.2
  219.7 26.2 %collective-permute-done = bf16[128,8192]{1,0:T(8,128)(2,1)S(1)} collective-permute-done((bf16[128,8192]{1,0:T(8,128)(2,1)}, bf16[128,8192]{1,0:T(8,128)(2,1)S(1)}, u32[]{:S(2)}, u32[]{:S(2)}) %collective-permute-start) | collective-permute-done | bytes 2097184 | tf_op jit(solution)/shard_map/while/body/eval_jaxpr/ppermute | solution.py:13
  246.0 1.6 conditional.2
  248.8 26.2 %collective-permute-done = bf16[128,8192]{1,0:T(8,128)(2,1)S(1)} collective-permute-done((bf16[128,8192]{1,0:T(8,128)(2,1)}, bf16[128,8192]{1,0:T(8,128)(2,1)S(1)}, u32[]{:S(2)}, u32[]{:S(2)}) %collective-permute-start) | collective-permute-done | bytes 2097184 | tf_op jit(solution)/shard_map/while/body/eval_jaxpr/ppermute | solution.py:13
  275.1 1.6 conditional.2
  277.9 26.2 %collective-permute-done = bf16[128,8192]{1,0:T(8,128)(2,1)S(1)} collective-permute-done((bf16[128,8192]{1,0:T(8,128)(2,1)}, bf16[128,8192]{1,0:T(8,128)(2,1)S(1)}, u32[]{:S(2)}, u32[]{:S(2)}) %collective-permute-start) | collective-permute-done | bytes 2097184 | tf_op jit(solution)/shard_map/while/body/eval_jaxpr/ppermute | solution.py:13
  304.2 1.6 conditional.2
  307.0 26.2 %collective-permute-done = bf16[128,8192]{1,0:T(8,128)(2,1)S(1)} collective-permute-done((bf16[128,8192]{1,0:T(8,128)(2,1)}, bf16[128,8192]{1,0:T(8,128)(2,1)S(1)}, u32[]{:S(2)}, u32[]{:S(2)}) %collective-permute-start) | collective-permute-done | bytes 2097184 | tf_op jit(solution)/shard_map/while/body/eval_jaxpr/ppermute | solution.py:13
  333.3 1.6 conditional.2
  336.1 26.2 %collective-permute-done = bf16[128,8192]{1,0:T(8,128)(2,1)S(1)} collective-permute-done((bf16[128,8192]{1,0:T(8,128)(2,1)}, bf16[128,8192]{1,0:T(8,128)(2,1)S(1)}, u32[]{:S(2)}, u32[]{:S(2)}) %collective-permute-start) | collective-permute-done | bytes 2097184 | tf_op jit(solution)/shard_map/while/body/eval_jaxpr/ppermute | solution.py:13
  362.4 1.6 conditional.2
  365.2 26.2 %collective-permute-done = bf16[128,8192]{1,0:T(8,128)(2,1)S(1)} collective-permute-done((bf16[128,8192]{1,0:T(8,128)(2,1)}, bf16[128,8192]{1,0:T(8,128)(2,1)S(1)}, u32[]{:S(2)}, u32[]{:S(2)}) %collective-permute-start) | collective-permute-done | bytes 2097184 | tf_op jit(solution)/shard_map/while/body/eval_jaxpr/ppermute | solution.py:13
  391.5 1.6 conditional.2
  394.3 26.2 %collective-permute-done = bf16[128,8192]{1,0:T(8,128)(2,1)S(1)} collective-permute-done((bf16[128,8192]{1,0:T(8,128)(2,1)}, bf16[128,8192]{1,0:T(8,128)(2,1)S(1)}, u32[]{:S(2)}, u32[]{:S(2)}) %collective-permute-start) | collective-permute-done | bytes 2097184 | tf_op jit(solution)/shard_map/while/body/eval_jaxpr/ppermute | solution.py:13
  420.6 1.6 conditional.2
  423.4 26.2 %collective-permute-done = bf16[128,8192]{1,0:T(8,128)(2,1)S(1)} collective-permute-done((bf16[128,8192]{1,0:T(8,128)(2,1)}, bf16[128,8192]{1,0:T(8,128)(2,1)S(1)}, u32[]{:S(2)}, u32[]{:S(2)}) %collective-permute-start) | collective-permute-done | bytes 2097184 | tf_op jit(solution)/shard_map/while/body/eval_jaxpr/ppermute | solution.py:13
  449.7 1.6 conditional.2
  452.5 182.0 %collective-permute-done = bf16[128,8192]{1,0:T(8,128)(2,1)S(1)} collective-permute-done((bf16[128,8192]{1,0:T(8,128)(2,1)}, bf16[128,8192]{1,0:T(8,128)(2,1)S(1)}, u32[]{:S(2)}, u32[]{:S(2)}) %collective-permute-start) | collective-permute-done | bytes 2097184 | tf_op jit(solution)/shard_map/while/body/eval_jaxpr/ppermute | solution.py:13
  634.5 22.1 %conditional.2 = (bf16[128,8192]{1,0:T(8,128)(2,1)}, f32[128,32]{0,1:T(8,128)S(1)}) conditional(s32[]{:T(128)} %convert_element_type.46, () %tuple.54, (pred[]{:T(512)}, bf16[512,8192]{1,0:T(8,128)(2,1)}, s32[]{:T(128)}, bf16[128,8192]{1,0:T(8,128)(2,1)S(1)}, bf16[512,8192]{1,0:T(8,128)(2,1)}, /*index=5*/bf16[8192,512]{1,0:T(8,128)(2,1)}, s32[]{:T(128)}, ...), branch_computations={%region_1.1_spmd, %region_2.2_spmd} | conditional | flops 3368239104 | bytes 70828144 | solution.py:96
  634.5 2.5 dynamic-slice_select_fusion
  637.1 6.5 fusion.5
  643.6 4.2 fusion
  648.6 5.5 fusion.15
  654.0 2.4 fusion.1
  657.9 29.9 %collective-permute-done = bf16[128,8192]{1,0:T(8,128)(2,1)S(1)} collective-permute-done((bf16[128,8192]{1,0:T(8,128)(2,1)}, bf16[128,8192]{1,0:T(8,128)(2,1)S(1)}, u32[]{:S(2)}, u32[]{:S(2)}) %collective-permute-start) | collective-permute-done | bytes 2097184 | tf_op jit(solution)/shard_map/while/body/eval_jaxpr/ppermute | solution.py:13
  687.8 22.1 %conditional.2 = (bf16[128,8192]{1,0:T(8,128)(2,1)}, f32[128,32]{0,1:T(8,128)S(1)}) conditional(s32[]{:T(128)} %convert_element_type.46, () %tuple.54, (pred[]{:T(512)}, bf16[512,8192]{1,0:T(8,128)(2,1)}, s32[]{:T(128)}, bf16[128,8192]{1,0:T(8,128)(2,1)S(1)}, bf16[512,8192]{1,0:T(8,128)(2,1)}, /*index=5*/bf16[8192,512]{1,0:T(8,128)(2,1)}, s32[]{:T(128)}, ...), branch_computations={%region_1.1_spmd, %region_2.2_spmd} | conditional | flops 3368239104 | bytes 70828144 | solution.py:96
  687.8 2.5 dynamic-slice_select_fusion
  690.3 6.5 fusion.5
  696.8 4.2 fusion
  701.8 5.5 fusion.15
  707.3 2.4 fusion.1
  711.2 29.9 %collective-permute-done = bf16[128,8192]{1,0:T(8,128)(2,1)S(1)} collective-permute-done((bf16[128,8192]{1,0:T(8,128)(2,1)}, bf16[128,8192]{1,0:T(8,128)(2,1)S(1)}, u32[]{:S(2)}, u32[]{:S(2)}) %collective-permute-start) | collective-permute-done | bytes 2097184 | tf_op jit(solution)/shard_map/while/body/eval_jaxpr/ppermute | solution.py:13
  741.0 22.1 %conditional.2 = (bf16[128,8192]{1,0:T(8,128)(2,1)}, f32[128,32]{0,1:T(8,128)S(1)}) conditional(s32[]{:T(128)} %convert_element_type.46, () %tuple.54, (pred[]{:T(512)}, bf16[512,8192]{1,0:T(8,128)(2,1)}, s32[]{:T(128)}, bf16[128,8192]{1,0:T(8,128)(2,1)S(1)}, bf16[512,8192]{1,0:T(8,128)(2,1)}, /*index=5*/bf16[8192,512]{1,0:T(8,128)(2,1)}, s32[]{:T(128)}, ...), branch_computations={%region_1.1_spmd, %region_2.2_spmd} | conditional | flops 3368239104 | bytes 70828144 | solution.py:96
  741.0 2.5 dynamic-slice_select_fusion
  743.6 6.5 fusion.5
  750.1 4.2 fusion
  755.1 5.5 fusion.15
  760.5 2.4 fusion.1
  764.4 29.0 %collective-permute-done = bf16[128,8192]{1,0:T(8,128)(2,1)S(1)} collective-permute-done((bf16[128,8192]{1,0:T(8,128)(2,1)}, bf16[128,8192]{1,0:T(8,128)(2,1)S(1)}, u32[]{:S(2)}, u32[]{:S(2)}) %collective-permute-start) | collective-permute-done | bytes 2097184 | tf_op jit(solution)/shard_map/while/body/eval_jaxpr/ppermute | solution.py:13
  793.5 22.0 %conditional.2 = (bf16[128,8192]{1,0:T(8,128)(2,1)}, f32[128,32]{0,1:T(8,128)S(1)}) conditional(s32[]{:T(128)} %convert_element_type.46, () %tuple.54, (pred[]{:T(512)}, bf16[512,8192]{1,0:T(8,128)(2,1)}, s32[]{:T(128)}, bf16[128,8192]{1,0:T(8,128)(2,1)S(1)}, bf16[512,8192]{1,0:T(8,128)(2,1)}, /*index=5*/bf16[8192,512]{1,0:T(8,128)(2,1)}, s32[]{:T(128)}, ...), branch_computations={%region_1.1_spmd, %region_2.2_spmd} | conditional | flops 3368239104 | bytes 70828144 | solution.py:96
  793.5 2.5 dynamic-slice_select_fusion
  796.0 6.5 fusion.5
  802.5 4.2 fusion
  807.5 5.4 fusion.15
  812.9 2.4 fusion.1
  816.8 5.8 collective-permute-done
  823.2 2.6 compare_select_fusion.1
  826.0 86.6 %psum.7 = f32[4,32]{0,1:T(8,128)S(1)} all-reduce(f32[4,32]{0,1:T(8,128)S(1)} %reduce_sum.9), channel_id=1, replica_groups=mesh['dp'=8,'pipe'=16] {'pipe'}, use_global_device_ids=true, to_apply=%region_5.6 | all-reduce | flops 128 | bytes 1024 | tf_op jit(solution)/shard_map/psum | solution.py:113
  (121 shorter events, 54.2 us)
Async XLA Ops:
  0.0 32.6 %copy-start.2 = (bf16[1,4,8192]{2,1,0:T(4,128)(2,1)S(1)}, bf16[1,4,8192]{2,1,0:T(4,128)(2,1)}, u32[]{:S(2)}) copy-start(bf16[1,4,8192]{2,1,0:T(4,128)(2,1)} %param.21) | copy-start | bytes 196612
  63.3 0.8 copy-start
  63.3 0.8 copy-start.1
  64.1 758.5 %copy-start.3 = (s32[4]{0:T(128)S(1)}, s32[4]{0:T(128)}, u32[]{:S(2)}) copy-start(s32[4]{0:T(128)} %param.24) | copy-start | bytes 52
  64.1 848.5 %copy-start.4 = (s32[32]{0:T(128)S(1)}, s32[32]{0:T(128)}, u32[]{:S(2)}) copy-start(s32[32]{0:T(128)} %param.25) | copy-start | bytes 388
  65.7 6.3 collective-permute-start
  73.5 26.9 %collective-permute-start = (bf16[128,8192]{1,0:T(8,128)(2,1)}, bf16[128,8192]{1,0:T(8,128)(2,1)S(1)}, u32[]{:S(2)}, u32[]{:S(2)}) collective-permute-start(bf16[128,8192]{1,0:T(8,128)(2,1)} %get-tuple-element.491), channel_id=1, source_target_pairs={{1,0},{2,1},{3,2},{4,3},{5,4},{6,5},{7,6},{8,7},{9,8},{10,9},{11,1... | collective-permute-start | bytes 6291464 | tf_op jit(solution)/shard_map/while/body/eval_jaxpr/ppermute | solution.py:13
  102.0 27.6 %collective-permute-start = (bf16[128,8192]{1,0:T(8,128)(2,1)}, bf16[128,8192]{1,0:T(8,128)(2,1)S(1)}, u32[]{:S(2)}, u32[]{:S(2)}) collective-permute-start(bf16[128,8192]{1,0:T(8,128)(2,1)} %get-tuple-element.491), channel_id=1, source_target_pairs={{1,0},{2,1},{3,2},{4,3},{5,4},{6,5},{7,6},{8,7},{9,8},{10,9},{11,1... | collective-permute-start | bytes 6291464 | tf_op jit(solution)/shard_map/while/body/eval_jaxpr/ppermute | solution.py:13
  131.1 27.6 %collective-permute-start = (bf16[128,8192]{1,0:T(8,128)(2,1)}, bf16[128,8192]{1,0:T(8,128)(2,1)S(1)}, u32[]{:S(2)}, u32[]{:S(2)}) collective-permute-start(bf16[128,8192]{1,0:T(8,128)(2,1)} %get-tuple-element.491), channel_id=1, source_target_pairs={{1,0},{2,1},{3,2},{4,3},{5,4},{6,5},{7,6},{8,7},{9,8},{10,9},{11,1... | collective-permute-start | bytes 6291464 | tf_op jit(solution)/shard_map/while/body/eval_jaxpr/ppermute | solution.py:13
  160.2 27.6 %collective-permute-start = (bf16[128,8192]{1,0:T(8,128)(2,1)}, bf16[128,8192]{1,0:T(8,128)(2,1)S(1)}, u32[]{:S(2)}, u32[]{:S(2)}) collective-permute-start(bf16[128,8192]{1,0:T(8,128)(2,1)} %get-tuple-element.491), channel_id=1, source_target_pairs={{1,0},{2,1},{3,2},{4,3},{5,4},{6,5},{7,6},{8,7},{9,8},{10,9},{11,1... | collective-permute-start | bytes 6291464 | tf_op jit(solution)/shard_map/while/body/eval_jaxpr/ppermute | solution.py:13
  189.3 27.6 %collective-permute-start = (bf16[128,8192]{1,0:T(8,128)(2,1)}, bf16[128,8192]{1,0:T(8,128)(2,1)S(1)}, u32[]{:S(2)}, u32[]{:S(2)}) collective-permute-start(bf16[128,8192]{1,0:T(8,128)(2,1)} %get-tuple-element.491), channel_id=1, source_target_pairs={{1,0},{2,1},{3,2},{4,3},{5,4},{6,5},{7,6},{8,7},{9,8},{10,9},{11,1... | collective-permute-start | bytes 6291464 | tf_op jit(solution)/shard_map/while/body/eval_jaxpr/ppermute | solution.py:13
  218.4 27.6 %collective-permute-start = (bf16[128,8192]{1,0:T(8,128)(2,1)}, bf16[128,8192]{1,0:T(8,128)(2,1)S(1)}, u32[]{:S(2)}, u32[]{:S(2)}) collective-permute-start(bf16[128,8192]{1,0:T(8,128)(2,1)} %get-tuple-element.491), channel_id=1, source_target_pairs={{1,0},{2,1},{3,2},{4,3},{5,4},{6,5},{7,6},{8,7},{9,8},{10,9},{11,1... | collective-permute-start | bytes 6291464 | tf_op jit(solution)/shard_map/while/body/eval_jaxpr/ppermute | solution.py:13
  247.5 27.6 %collective-permute-start = (bf16[128,8192]{1,0:T(8,128)(2,1)}, bf16[128,8192]{1,0:T(8,128)(2,1)S(1)}, u32[]{:S(2)}, u32[]{:S(2)}) collective-permute-start(bf16[128,8192]{1,0:T(8,128)(2,1)} %get-tuple-element.491), channel_id=1, source_target_pairs={{1,0},{2,1},{3,2},{4,3},{5,4},{6,5},{7,6},{8,7},{9,8},{10,9},{11,1... | collective-permute-start | bytes 6291464 | tf_op jit(solution)/shard_map/while/body/eval_jaxpr/ppermute | solution.py:13
  276.6 27.6 %collective-permute-start = (bf16[128,8192]{1,0:T(8,128)(2,1)}, bf16[128,8192]{1,0:T(8,128)(2,1)S(1)}, u32[]{:S(2)}, u32[]{:S(2)}) collective-permute-start(bf16[128,8192]{1,0:T(8,128)(2,1)} %get-tuple-element.491), channel_id=1, source_target_pairs={{1,0},{2,1},{3,2},{4,3},{5,4},{6,5},{7,6},{8,7},{9,8},{10,9},{11,1... | collective-permute-start | bytes 6291464 | tf_op jit(solution)/shard_map/while/body/eval_jaxpr/ppermute | solution.py:13
  305.7 27.6 %collective-permute-start = (bf16[128,8192]{1,0:T(8,128)(2,1)}, bf16[128,8192]{1,0:T(8,128)(2,1)S(1)}, u32[]{:S(2)}, u32[]{:S(2)}) collective-permute-start(bf16[128,8192]{1,0:T(8,128)(2,1)} %get-tuple-element.491), channel_id=1, source_target_pairs={{1,0},{2,1},{3,2},{4,3},{5,4},{6,5},{7,6},{8,7},{9,8},{10,9},{11,1... | collective-permute-start | bytes 6291464 | tf_op jit(solution)/shard_map/while/body/eval_jaxpr/ppermute | solution.py:13
  334.8 27.6 %collective-permute-start = (bf16[128,8192]{1,0:T(8,128)(2,1)}, bf16[128,8192]{1,0:T(8,128)(2,1)S(1)}, u32[]{:S(2)}, u32[]{:S(2)}) collective-permute-start(bf16[128,8192]{1,0:T(8,128)(2,1)} %get-tuple-element.491), channel_id=1, source_target_pairs={{1,0},{2,1},{3,2},{4,3},{5,4},{6,5},{7,6},{8,7},{9,8},{10,9},{11,1... | collective-permute-start | bytes 6291464 | tf_op jit(solution)/shard_map/while/body/eval_jaxpr/ppermute | solution.py:13
  363.9 27.6 %collective-permute-start = (bf16[128,8192]{1,0:T(8,128)(2,1)}, bf16[128,8192]{1,0:T(8,128)(2,1)S(1)}, u32[]{:S(2)}, u32[]{:S(2)}) collective-permute-start(bf16[128,8192]{1,0:T(8,128)(2,1)} %get-tuple-element.491), channel_id=1, source_target_pairs={{1,0},{2,1},{3,2},{4,3},{5,4},{6,5},{7,6},{8,7},{9,8},{10,9},{11,1... | collective-permute-start | bytes 6291464 | tf_op jit(solution)/shard_map/while/body/eval_jaxpr/ppermute | solution.py:13
  393.0 27.6 %collective-permute-start = (bf16[128,8192]{1,0:T(8,128)(2,1)}, bf16[128,8192]{1,0:T(8,128)(2,1)S(1)}, u32[]{:S(2)}, u32[]{:S(2)}) collective-permute-start(bf16[128,8192]{1,0:T(8,128)(2,1)} %get-tuple-element.491), channel_id=1, source_target_pairs={{1,0},{2,1},{3,2},{4,3},{5,4},{6,5},{7,6},{8,7},{9,8},{10,9},{11,1... | collective-permute-start | bytes 6291464 | tf_op jit(solution)/shard_map/while/body/eval_jaxpr/ppermute | solution.py:13
  422.1 27.6 %collective-permute-start = (bf16[128,8192]{1,0:T(8,128)(2,1)}, bf16[128,8192]{1,0:T(8,128)(2,1)S(1)}, u32[]{:S(2)}, u32[]{:S(2)}) collective-permute-start(bf16[128,8192]{1,0:T(8,128)(2,1)} %get-tuple-element.491), channel_id=1, source_target_pairs={{1,0},{2,1},{3,2},{4,3},{5,4},{6,5},{7,6},{8,7},{9,8},{10,9},{11,1... | collective-permute-start | bytes 6291464 | tf_op jit(solution)/shard_map/while/body/eval_jaxpr/ppermute | solution.py:13
  451.2 183.3 %collective-permute-start = (bf16[128,8192]{1,0:T(8,128)(2,1)}, bf16[128,8192]{1,0:T(8,128)(2,1)S(1)}, u32[]{:S(2)}, u32[]{:S(2)}) collective-permute-start(bf16[128,8192]{1,0:T(8,128)(2,1)} %get-tuple-element.491), channel_id=1, source_target_pairs={{1,0},{2,1},{3,2},{4,3},{5,4},{6,5},{7,6},{8,7},{9,8},{10,9},{11,1... | collective-permute-start | bytes 6291464 | tf_op jit(solution)/shard_map/while/body/eval_jaxpr/ppermute | solution.py:13
  634.5 9.0 slice-start
  637.0 6.5 slice-start.1
  656.6 31.2 %collective-permute-start = (bf16[128,8192]{1,0:T(8,128)(2,1)}, bf16[128,8192]{1,0:T(8,128)(2,1)S(1)}, u32[]{:S(2)}, u32[]{:S(2)}) collective-permute-start(bf16[128,8192]{1,0:T(8,128)(2,1)} %get-tuple-element.491), channel_id=1, source_target_pairs={{1,0},{2,1},{3,2},{4,3},{5,4},{6,5},{7,6},{8,7},{9,8},{10,9},{11,1... | collective-permute-start | bytes 6291464 | tf_op jit(solution)/shard_map/while/body/eval_jaxpr/ppermute | solution.py:13
  687.8 9.0 slice-start
  690.3 6.5 slice-start.1
  709.8 31.2 %collective-permute-start = (bf16[128,8192]{1,0:T(8,128)(2,1)}, bf16[128,8192]{1,0:T(8,128)(2,1)S(1)}, u32[]{:S(2)}, u32[]{:S(2)}) collective-permute-start(bf16[128,8192]{1,0:T(8,128)(2,1)} %get-tuple-element.491), channel_id=1, source_target_pairs={{1,0},{2,1},{3,2},{4,3},{5,4},{6,5},{7,6},{8,7},{9,8},{10,9},{11,1... | collective-permute-start | bytes 6291464 | tf_op jit(solution)/shard_map/while/body/eval_jaxpr/ppermute | solution.py:13
  741.0 9.0 slice-start
  743.6 6.5 slice-start.1
  763.1 30.4 %collective-permute-start = (bf16[128,8192]{1,0:T(8,128)(2,1)}, bf16[128,8192]{1,0:T(8,128)(2,1)S(1)}, u32[]{:S(2)}, u32[]{:S(2)}) collective-permute-start(bf16[128,8192]{1,0:T(8,128)(2,1)} %get-tuple-element.491), channel_id=1, source_target_pairs={{1,0},{2,1},{3,2},{4,3},{5,4},{6,5},{7,6},{8,7},{9,8},{10,9},{11,1... | collective-permute-start | bytes 6291464 | tf_op jit(solution)/shard_map/while/body/eval_jaxpr/ppermute | solution.py:13
  793.5 9.0 slice-start
  796.0 6.5 slice-start.1
  815.4 7.2 collective-permute-start
where the time goes:
time: 914 us; the launch traced here: 913 us
  waiting for transfers between devices  622 us (68%)
  blocking collectives  148 us (16%)
  matrix products  77.8 us (9%)
  local copies, waits for them, and re-layouts  27.1 us (3%)
  starting transfers between devices  24.4 us (3%)
  other arithmetic  13.2 us (1%)
    ppermute x19, waiting for transfers between devices, from_behind(): lax.ppermute(value, axis, [(source, source + steps) for source in range(f...  622 us
    psum x1, blocking collectives, local(): totals = lax.psum(local_sums, 'pipe') * SLOT ** (-0.5)  86.6 us
    all_gather x1, blocking collectives, local(): lax.all_gather(value_rows[0], 'dp', axis=0, tiled=True)  31.1 us
    all_gather x1, blocking collectives, local(): lax.all_gather(input_rows[0], 'dp', axis=0, tiled=True)  30.5 us
    dot_general x4, matrix products, compute(): jnp.einsum('td,rd->tr', gradient_leaving, up_map, preferred_element_type=...  25.8 us
    ppermute x19, starting transfers between devices, from_behind(): lax.ppermute(value, axis, [(source, source + steps) for source in range(f...  24.4 us
    another operation x31, local copies, waits for them, and re-layouts  23.5 us
    dot_general x4, matrix products, compute(): jnp.einsum('tr,qr->tq', hidden, hid_factor, preferred_element_type=jnp.fl...  21.8 us
  transfers between devices with their start and end apart: 19, of which 19 were waited for; matrix products, arithmetic and copies ran while one was open for 0% of the time, Pallas kernels for 0%

commit v1 on v0

--- a/solution.py
+++ b/solution.py
@@ -110,7 +110,7 @@
     )
     masked = per_token * live_mask[:, None]
     local_sums = jnp.sum(masked.reshape(ex_dev, SLOT, query_total), axis=1)
-    totals = lax.psum(local_sums, "pipe") * SLOT ** (-0.5)
+    totals = jnp.sum(jax.lax.all_gather(local_sums, axis_name="pipe"), axis=0) * SLOT ** (-0.5)
     example_ids = lax.axis_index("dp") * ex_dev + lax.broadcasted_iota(jnp.int32, (ex_dev,), 0)
     keep_mask = (example_ids[:, None] != query_example[None, :]).astype(jnp.float32)
     return totals * keep_mask

time: 914 us -> 869 us (0.951)
  blocking collectives: 148 us -> 102 us
    psum x1 -> x0, blocking collectives: 86.6 us -> none  [local(): totals = lax.psum(local_sums, 'pipe') * SLOT ** (-0.5)]
    all_gather x0 -> x1, blocking collectives: none -> 40.8 us  [local(): jax.lax.all_gather(local_sums, axis_name='pipe')]
where the time goes in v1:
time: 869 us; the launch traced here: 868 us
  waiting for transfers between devices  622 us (72%)
  blocking collectives  102 us (12%)
  matrix products  77.8 us (9%)
  local copies, waits for them, and re-layouts  26.5 us (3%)
  starting transfers between devices  24.4 us (3%)
  other arithmetic  13.8 us (2%)
    ppermute x19, waiting for transfers between devices, from_behind(): lax.ppermute(value, axis, [(source, source + steps) for source in range(f...  622 us
    all_gather x1, blocking collectives, local(): jax.lax.all_gather(local_sums, axis_name='pipe')  40.8 us
    all_gather x1, blocking collectives, local(): lax.all_gather(value_rows[0], 'dp', axis=0, tiled=True)  31.1 us
    all_gather x1, blocking collectives, local(): lax.all_gather(input_rows[0], 'dp', axis=0, tiled=True)  30.5 us
    dot_general x4, matrix products, compute(): jnp.einsum('td,rd->tr', gradient_leaving, up_map, preferred_element_type=...  25.8 us
    ppermute x19, starting transfers between devices, from_behind(): lax.ppermute(value, axis, [(source, source + steps) for source in range(f...  24.4 us
    another operation x31, local copies, waits for them, and re-layouts  23.5 us
    dot_general x4, matrix products, compute(): jnp.einsum('tr,qr->tq', hidden, hid_factor, preferred_element_type=jnp.fl...  21.8 us
  transfers between devices with their start and end apart: 19, of which 19 were waited for; matrix products, arithmetic and copies ran while one was open for 0% of the time, Pallas kernels for 0%

profile of v1, /device:TPU:8, one launch (start us, length us, event | category | flops | bytes accessed | tf_op | source)
XLA Modules:
  0.0 867.6 jit_solution(6736437613618303772)
XLA Ops:
  1.0 31.1 %all-gather = bf16[1,32,8192]{2,0,1:T(2,128)(2,1)S(1)} all-gather(bf16[1,4,8192]{2,0,1:T(2,128)(2,1)S(1)} %copy.14), channel_id=2, replica_groups=mesh['dp'=8,'pipe'=16] {'dp'}, dimensions={1}, use_global_device_ids=true | all-gather | bytes 589824 | tf_op jit(solution)/shard_map/all_gather | solution.py:34
  32.7 30.5 %all-gather.1 = bf16[1,32,8192]{2,0,1:T(2,128)(2,1)S(1)} all-gather(bf16[1,4,8192]{2,0,1:T(2,128)(2,1)S(1)} %copy.15), channel_id=3, replica_groups=mesh['dp'=8,'pipe'=16] {'dp'}, dimensions={1}, use_global_device_ids=true | all-gather | bytes 589824 | tf_op jit(solution)/shard_map/all_gather | solution.py:35
  64.1 758.5 %while.18 = (s32[]{:T(128)}, bf16[128,8192]{1,0:T(8,128)(2,1)S(1)}, f32[512,32]{0,1:T(8,128)S(1)}, s32[]{:T(128)}, pred[]{:T(512)}, /*index=5*/bf16[512,8192]{1,...) while((s32[]{:T(128)}, bf16[128,8192]{1,0:T(8,128)(2,1)S(1)}, ...), condition=%wide.region_3.4_spmd, body=%wide.region_0.3_spmd.sunk | while | flops 3368243200 | bytes 79266320 | solution.py:106
  64.1 1.6 conditional.2
  64.2 1.5 broadcast.142
  67.0 4.9 collective-permute-done
  72.0 1.6 conditional.2
  74.8 25.6 %collective-permute-done = bf16[128,8192]{1,0:T(8,128)(2,1)S(1)} collective-permute-done((bf16[128,8192]{1,0:T(8,128)(2,1)}, bf16[128,8192]{1,0:T(8,128)(2,1)S(1)}, u32[]{:S(2)}, u32[]{:S(2)}) %collective-permute-start) | collective-permute-done | bytes 2097184 | tf_op jit(solution)/shard_map/while/body/eval_jaxpr/ppermute | solution.py:13
  100.4 1.6 conditional.2
  103.3 26.2 %collective-permute-done = bf16[128,8192]{1,0:T(8,128)(2,1)S(1)} collective-permute-done((bf16[128,8192]{1,0:T(8,128)(2,1)}, bf16[128,8192]{1,0:T(8,128)(2,1)S(1)}, u32[]{:S(2)}, u32[]{:S(2)}) %collective-permute-start) | collective-permute-done | bytes 2097184 | tf_op jit(solution)/shard_map/while/body/eval_jaxpr/ppermute | solution.py:13
  129.5 1.6 conditional.2
  132.4 26.2 %collective-permute-done = bf16[128,8192]{1,0:T(8,128)(2,1)S(1)} collective-permute-done((bf16[128,8192]{1,0:T(8,128)(2,1)}, bf16[128,8192]{1,0:T(8,128)(2,1)S(1)}, u32[]{:S(2)}, u32[]{:S(2)}) %collective-permute-start) | collective-permute-done | bytes 2097184 | tf_op jit(solution)/shard_map/while/body/eval_jaxpr/ppermute | solution.py:13
  158.6 1.6 conditional.2
  161.5 26.2 %collective-permute-done = bf16[128,8192]{1,0:T(8,128)(2,1)S(1)} collective-permute-done((bf16[128,8192]{1,0:T(8,128)(2,1)}, bf16[128,8192]{1,0:T(8,128)(2,1)S(1)}, u32[]{:S(2)}, u32[]{:S(2)}) %collective-permute-start) | collective-permute-done | bytes 2097184 | tf_op jit(solution)/shard_map/while/body/eval_jaxpr/ppermute | solution.py:13
  187.7 1.6 conditional.2
  190.6 26.2 %collective-permute-done = bf16[128,8192]{1,0:T(8,128)(2,1)S(1)} collective-permute-done((bf16[128,8192]{1,0:T(8,128)(2,1)}, bf16[128,8192]{1,0:T(8,128)(2,1)S(1)}, u32[]{:S(2)}, u32[]{:S(2)}) %collective-permute-start) | collective-permute-done | bytes 2097184 | tf_op jit(solution)/shard_map/while/body/eval_jaxpr/ppermute | solution.py:13
  216.9 1.6 conditional.2
  219.7 26.2 %collective-permute-done = bf16[128,8192]{1,0:T(8,128)(2,1)S(1)} collective-permute-done((bf16[128,8192]{1,0:T(8,128)(2,1)}, bf16[128,8192]{1,0:T(8,128)(2,1)S(1)}, u32[]{:S(2)}, u32[]{:S(2)}) %collective-permute-start) | collective-permute-done | bytes 2097184 | tf_op jit(solution)/shard_map/while/body/eval_jaxpr/ppermute | solution.py:13
  246.0 1.6 conditional.2
  248.8 26.2 %collective-permute-done = bf16[128,8192]{1,0:T(8,128)(2,1)S(1)} collective-permute-done((bf16[128,8192]{1,0:T(8,128)(2,1)}, bf16[128,8192]{1,0:T(8,128)(2,1)S(1)}, u32[]{:S(2)}, u32[]{:S(2)}) %collective-permute-start) | collective-permute-done | bytes 2097184 | tf_op jit(solution)/shard_map/while/body/eval_jaxpr/ppermute | solution.py:13
  275.1 1.6 conditional.2
  277.9 26.2 %collective-permute-done = bf16[128,8192]{1,0:T(8,128)(2,1)S(1)} collective-permute-done((bf16[128,8192]{1,0:T(8,128)(2,1)}, bf16[128,8192]{1,0:T(8,128)(2,1)S(1)}, u32[]{:S(2)}, u32[]{:S(2)}) %collective-permute-start) | collective-permute-done | bytes 2097184 | tf_op jit(solution)/shard_map/while/body/eval_jaxpr/ppermute | solution.py:13
  304.2 1.6 conditional.2
  307.0 26.2 %collective-permute-done = bf16[128,8192]{1,0:T(8,128)(2,1)S(1)} collective-permute-done((bf16[128,8192]{1,0:T(8,128)(2,1)}, bf16[128,8192]{1,0:T(8,128)(2,1)S(1)}, u32[]{:S(2)}, u32[]{:S(2)}) %collective-permute-start) | collective-permute-done | bytes 2097184 | tf_op jit(solution)/shard_map/while/body/eval_jaxpr/ppermute | solution.py:13
  333.3 1.6 conditional.2
  336.1 26.2 %collective-permute-done = bf16[128,8192]{1,0:T(8,128)(2,1)S(1)} collective-permute-done((bf16[128,8192]{1,0:T(8,128)(2,1)}, bf16[128,8192]{1,0:T(8,128)(2,1)S(1)}, u32[]{:S(2)}, u32[]{:S(2)}) %collective-permute-start) | collective-permute-done | bytes 2097184 | tf_op jit(solution)/shard_map/while/body/eval_jaxpr/ppermute | solution.py:13
  362.4 1.6 conditional.2
  365.2 26.2 %collective-permute-done = bf16[128,8192]{1,0:T(8,128)(2,1)S(1)} collective-permute-done((bf16[128,8192]{1,0:T(8,128)(2,1)}, bf16[128,8192]{1,0:T(8,128)(2,1)S(1)}, u32[]{:S(2)}, u32[]{:S(2)}) %collective-permute-start) | collective-permute-done | bytes 2097184 | tf_op jit(solution)/shard_map/while/body/eval_jaxpr/ppermute | solution.py:13
  391.5 1.6 conditional.2
  394.3 26.2 %collective-permute-done = bf16[128,8192]{1,0:T(8,128)(2,1)S(1)} collective-permute-done((bf16[128,8192]{1,0:T(8,128)(2,1)}, bf16[128,8192]{1,0:T(8,128)(2,1)S(1)}, u32[]{:S(2)}, u32[]{:S(2)}) %collective-permute-start) | collective-permute-done | bytes 2097184 | tf_op jit(solution)/shard_map/while/body/eval_jaxpr/ppermute | solution.py:13
  420.6 1.6 conditional.2
  423.4 26.2 %collective-permute-done = bf16[128,8192]{1,0:T(8,128)(2,1)S(1)} collective-permute-done((bf16[128,8192]{1,0:T(8,128)(2,1)}, bf16[128,8192]{1,0:T(8,128)(2,1)S(1)}, u32[]{:S(2)}, u32[]{:S(2)}) %collective-permute-start) | collective-permute-done | bytes 2097184 | tf_op jit(solution)/shard_map/while/body/eval_jaxpr/ppermute | solution.py:13
  449.7 1.6 conditional.2
  452.5 182.0 %collective-permute-done = bf16[128,8192]{1,0:T(8,128)(2,1)S(1)} collective-permute-done((bf16[128,8192]{1,0:T(8,128)(2,1)}, bf16[128,8192]{1,0:T(8,128)(2,1)S(1)}, u32[]{:S(2)}, u32[]{:S(2)}) %collective-permute-start) | collective-permute-done | bytes 2097184 | tf_op jit(solution)/shard_map/while/body/eval_jaxpr/ppermute | solution.py:13
  634.5 22.1 %conditional.2 = (bf16[128,8192]{1,0:T(8,128)(2,1)}, f32[128,32]{0,1:T(8,128)S(1)}) conditional(s32[]{:T(128)} %convert_element_type.46, () %tuple.54, (pred[]{:T(512)}, bf16[512,8192]{1,0:T(8,128)(2,1)}, s32[]{:T(128)}, bf16[128,8192]{1,0:T(8,128)(2,1)S(1)}, bf16[512,8192]{1,0:T(8,128)(2,1)}, /*index=5*/bf16[8192,512]{1,0:T(8,128)(2,1)}, s32[]{:T(128)}, ...), branch_computations={%region_1.1_spmd, %region_2.2_spmd} | conditional | flops 3368239104 | bytes 70828144 | solution.py:96
  634.5 2.5 dynamic-slice_select_fusion
  637.1 6.5 fusion.5
  643.6 4.2 fusion
  648.6 5.5 fusion.15
  654.0 2.4 fusion.1
  657.9 29.9 %collective-permute-done = bf16[128,8192]{1,0:T(8,128)(2,1)S(1)} collective-permute-done((bf16[128,8192]{1,0:T(8,128)(2,1)}, bf16[128,8192]{1,0:T(8,128)(2,1)S(1)}, u32[]{:S(2)}, u32[]{:S(2)}) %collective-permute-start) | collective-permute-done | bytes 2097184 | tf_op jit(solution)/shard_map/while/body/eval_jaxpr/ppermute | solution.py:13
  687.8 22.1 %conditional.2 = (bf16[128,8192]{1,0:T(8,128)(2,1)}, f32[128,32]{0,1:T(8,128)S(1)}) conditional(s32[]{:T(128)} %convert_element_type.46, () %tuple.54, (pred[]{:T(512)}, bf16[512,8192]{1,0:T(8,128)(2,1)}, s32[]{:T(128)}, bf16[128,8192]{1,0:T(8,128)(2,1)S(1)}, bf16[512,8192]{1,0:T(8,128)(2,1)}, /*index=5*/bf16[8192,512]{1,0:T(8,128)(2,1)}, s32[]{:T(128)}, ...), branch_computations={%region_1.1_spmd, %region_2.2_spmd} | conditional | flops 3368239104 | bytes 70828144 | solution.py:96
  687.8 2.5 dynamic-slice_select_fusion
  690.3 6.5 fusion.5
  696.8 4.2 fusion
  701.8 5.5 fusion.15
  707.3 2.4 fusion.1
  711.2 29.9 %collective-permute-done = bf16[128,8192]{1,0:T(8,128)(2,1)S(1)} collective-permute-done((bf16[128,8192]{1,0:T(8,128)(2,1)}, bf16[128,8192]{1,0:T(8,128)(2,1)S(1)}, u32[]{:S(2)}, u32[]{:S(2)}) %collective-permute-start) | collective-permute-done | bytes 2097184 | tf_op jit(solution)/shard_map/while/body/eval_jaxpr/ppermute | solution.py:13
  741.0 22.1 %conditional.2 = (bf16[128,8192]{1,0:T(8,128)(2,1)}, f32[128,32]{0,1:T(8,128)S(1)}) conditional(s32[]{:T(128)} %convert_element_type.46, () %tuple.54, (pred[]{:T(512)}, bf16[512,8192]{1,0:T(8,128)(2,1)}, s32[]{:T(128)}, bf16[128,8192]{1,0:T(8,128)(2,1)S(1)}, bf16[512,8192]{1,0:T(8,128)(2,1)}, /*index=5*/bf16[8192,512]{1,0:T(8,128)(2,1)}, s32[]{:T(128)}, ...), branch_computations={%region_1.1_spmd, %region_2.2_spmd} | conditional | flops 3368239104 | bytes 70828144 | solution.py:96
  741.0 2.5 dynamic-slice_select_fusion
  743.6 6.5 fusion.5
  750.1 4.2 fusion
  755.1 5.5 fusion.15
  760.5 2.4 fusion.1
  764.4 29.0 %collective-permute-done = bf16[128,8192]{1,0:T(8,128)(2,1)S(1)} collective-permute-done((bf16[128,8192]{1,0:T(8,128)(2,1)}, bf16[128,8192]{1,0:T(8,128)(2,1)S(1)}, u32[]{:S(2)}, u32[]{:S(2)}) %collective-permute-start) | collective-permute-done | bytes 2097184 | tf_op jit(solution)/shard_map/while/body/eval_jaxpr/ppermute | solution.py:13
  793.5 22.0 %conditional.2 = (bf16[128,8192]{1,0:T(8,128)(2,1)}, f32[128,32]{0,1:T(8,128)S(1)}) conditional(s32[]{:T(128)} %convert_element_type.46, () %tuple.54, (pred[]{:T(512)}, bf16[512,8192]{1,0:T(8,128)(2,1)}, s32[]{:T(128)}, bf16[128,8192]{1,0:T(8,128)(2,1)S(1)}, bf16[512,8192]{1,0:T(8,128)(2,1)}, /*index=5*/bf16[8192,512]{1,0:T(8,128)(2,1)}, s32[]{:T(128)}, ...), branch_computations={%region_1.1_spmd, %region_2.2_spmd} | conditional | flops 3368239104 | bytes 70828144 | solution.py:96
  793.5 2.5 dynamic-slice_select_fusion
  796.0 6.5 fusion.5
  802.5 4.2 fusion
  807.5 5.4 fusion.15
  812.9 2.4 fusion.1
  816.8 5.8 collective-permute-done
  823.2 2.6 compare_select_fusion.1
  826.1 40.8 %all-gather.3 = f32[16,4,32]{2,1,0:T(4,128)S(1)} all-gather(f32[1,4,32]{2,1,0:T(4,128)S(1)} %bitcast.53), channel_id=4, replica_groups=mesh['dp'=8,'pipe'=16] {'pipe'}, dimensions={0}, use_global_device_ids=true | all-gather | bytes 8704 | tf_op jit(solution)/shard_map/all_gather | solution.py:113
  (122 shorter events, 54.3 us)
Async XLA Ops:
  0.0 32.6 %copy-start.2 = (bf16[1,4,8192]{2,1,0:T(4,128)(2,1)S(1)}, bf16[1,4,8192]{2,1,0:T(4,128)(2,1)}, u32[]{:S(2)}) copy-start(bf16[1,4,8192]{2,1,0:T(4,128)(2,1)} %param.21) | copy-start | bytes 196612
  63.3 0.8 copy-start
  63.3 0.8 copy-start.1
  64.1 758.5 %copy-start.3 = (s32[4]{0:T(128)S(1)}, s32[4]{0:T(128)}, u32[]{:S(2)}) copy-start(s32[4]{0:T(128)} %param.24) | copy-start | bytes 52
  64.1 802.8 %copy-start.4 = (s32[32]{0:T(128)S(1)}, s32[32]{0:T(128)}, u32[]{:S(2)}) copy-start(s32[32]{0:T(128)} %param.25) | copy-start | bytes 388
  65.7 6.3 collective-permute-start
  73.5 26.9 %collective-permute-start = (bf16[128,8192]{1,0:T(8,128)(2,1)}, bf16[128,8192]{1,0:T(8,128)(2,1)S(1)}, u32[]{:S(2)}, u32[]{:S(2)}) collective-permute-start(bf16[128,8192]{1,0:T(8,128)(2,1)} %get-tuple-element.491), channel_id=1, source_target_pairs={{1,0},{2,1},{3,2},{4,3},{5,4},{6,5},{7,6},{8,7},{9,8},{10,9},{11,1... | collective-permute-start | bytes 6291464 | tf_op jit(solution)/shard_map/while/body/eval_jaxpr/ppermute | solution.py:13
  102.0 27.6 %collective-permute-start = (bf16[128,8192]{1,0:T(8,128)(2,1)}, bf16[128,8192]{1,0:T(8,128)(2,1)S(1)}, u32[]{:S(2)}, u32[]{:S(2)}) collective-permute-start(bf16[128,8192]{1,0:T(8,128)(2,1)} %get-tuple-element.491), channel_id=1, source_target_pairs={{1,0},{2,1},{3,2},{4,3},{5,4},{6,5},{7,6},{8,7},{9,8},{10,9},{11,1... | collective-permute-start | bytes 6291464 | tf_op jit(solution)/shard_map/while/body/eval_jaxpr/ppermute | solution.py:13
  131.1 27.6 %collective-permute-start = (bf16[128,8192]{1,0:T(8,128)(2,1)}, bf16[128,8192]{1,0:T(8,128)(2,1)S(1)}, u32[]{:S(2)}, u32[]{:S(2)}) collective-permute-start(bf16[128,8192]{1,0:T(8,128)(2,1)} %get-tuple-element.491), channel_id=1, source_target_pairs={{1,0},{2,1},{3,2},{4,3},{5,4},{6,5},{7,6},{8,7},{9,8},{10,9},{11,1... | collective-permute-start | bytes 6291464 | tf_op jit(solution)/shard_map/while/body/eval_jaxpr/ppermute | solution.py:13
  160.2 27.6 %collective-permute-start = (bf16[128,8192]{1,0:T(8,128)(2,1)}, bf16[128,8192]{1,0:T(8,128)(2,1)S(1)}, u32[]{:S(2)}, u32[]{:S(2)}) collective-permute-start(bf16[128,8192]{1,0:T(8,128)(2,1)} %get-tuple-element.491), channel_id=1, source_target_pairs={{1,0},{2,1},{3,2},{4,3},{5,4},{6,5},{7,6},{8,7},{9,8},{10,9},{11,1... | collective-permute-start | bytes 6291464 | tf_op jit(solution)/shard_map/while/body/eval_jaxpr/ppermute | solution.py:13
  189.3 27.6 %collective-permute-start = (bf16[128,8192]{1,0:T(8,128)(2,1)}, bf16[128,8192]{1,0:T(8,128)(2,1)S(1)}, u32[]{:S(2)}, u32[]{:S(2)}) collective-permute-start(bf16[128,8192]{1,0:T(8,128)(2,1)} %get-tuple-element.491), channel_id=1, source_target_pairs={{1,0},{2,1},{3,2},{4,3},{5,4},{6,5},{7,6},{8,7},{9,8},{10,9},{11,1... | collective-permute-start | bytes 6291464 | tf_op jit(solution)/shard_map/while/body/eval_jaxpr/ppermute | solution.py:13
  218.4 27.6 %collective-permute-start = (bf16[128,8192]{1,0:T(8,128)(2,1)}, bf16[128,8192]{1,0:T(8,128)(2,1)S(1)}, u32[]{:S(2)}, u32[]{:S(2)}) collective-permute-start(bf16[128,8192]{1,0:T(8,128)(2,1)} %get-tuple-element.491), channel_id=1, source_target_pairs={{1,0},{2,1},{3,2},{4,3},{5,4},{6,5},{7,6},{8,7},{9,8},{10,9},{11,1... | collective-permute-start | bytes 6291464 | tf_op jit(solution)/shard_map/while/body/eval_jaxpr/ppermute | solution.py:13
  247.5 27.6 %collective-permute-start = (bf16[128,8192]{1,0:T(8,128)(2,1)}, bf16[128,8192]{1,0:T(8,128)(2,1)S(1)}, u32[]{:S(2)}, u32[]{:S(2)}) collective-permute-start(bf16[128,8192]{1,0:T(8,128)(2,1)} %get-tuple-element.491), channel_id=1, source_target_pairs={{1,0},{2,1},{3,2},{4,3},{5,4},{6,5},{7,6},{8,7},{9,8},{10,9},{11,1... | collective-permute-start | bytes 6291464 | tf_op jit(solution)/shard_map/while/body/eval_jaxpr/ppermute | solution.py:13
  276.6 27.6 %collective-permute-start = (bf16[128,8192]{1,0:T(8,128)(2,1)}, bf16[128,8192]{1,0:T(8,128)(2,1)S(1)}, u32[]{:S(2)}, u32[]{:S(2)}) collective-permute-start(bf16[128,8192]{1,0:T(8,128)(2,1)} %get-tuple-element.491), channel_id=1, source_target_pairs={{1,0},{2,1},{3,2},{4,3},{5,4},{6,5},{7,6},{8,7},{9,8},{10,9},{11,1... | collective-permute-start | bytes 6291464 | tf_op jit(solution)/shard_map/while/body/eval_jaxpr/ppermute | solution.py:13
  305.7 27.6 %collective-permute-start = (bf16[128,8192]{1,0:T(8,128)(2,1)}, bf16[128,8192]{1,0:T(8,128)(2,1)S(1)}, u32[]{:S(2)}, u32[]{:S(2)}) collective-permute-start(bf16[128,8192]{1,0:T(8,128)(2,1)} %get-tuple-element.491), channel_id=1, source_target_pairs={{1,0},{2,1},{3,2},{4,3},{5,4},{6,5},{7,6},{8,7},{9,8},{10,9},{11,1... | collective-permute-start | bytes 6291464 | tf_op jit(solution)/shard_map/while/body/eval_jaxpr/ppermute | solution.py:13
  334.8 27.6 %collective-permute-start = (bf16[128,8192]{1,0:T(8,128)(2,1)}, bf16[128,8192]{1,0:T(8,128)(2,1)S(1)}, u32[]{:S(2)}, u32[]{:S(2)}) collective-permute-start(bf16[128,8192]{1,0:T(8,128)(2,1)} %get-tuple-element.491), channel_id=1, source_target_pairs={{1,0},{2,1},{3,2},{4,3},{5,4},{6,5},{7,6},{8,7},{9,8},{10,9},{11,1... | collective-permute-start | bytes 6291464 | tf_op jit(solution)/shard_map/while/body/eval_jaxpr/ppermute | solution.py:13
  363.9 27.6 %collective-permute-start = (bf16[128,8192]{1,0:T(8,128)(2,1)}, bf16[128,8192]{1,0:T(8,128)(2,1)S(1)}, u32[]{:S(2)}, u32[]{:S(2)}) collective-permute-start(bf16[128,8192]{1,0:T(8,128)(2,1)} %get-tuple-element.491), channel_id=1, source_target_pairs={{1,0},{2,1},{3,2},{4,3},{5,4},{6,5},{7,6},{8,7},{9,8},{10,9},{11,1... | collective-permute-start | bytes 6291464 | tf_op jit(solution)/shard_map/while/body/eval_jaxpr/ppermute | solution.py:13
  393.0 27.6 %collective-permute-start = (bf16[128,8192]{1,0:T(8,128)(2,1)}, bf16[128,8192]{1,0:T(8,128)(2,1)S(1)}, u32[]{:S(2)}, u32[]{:S(2)}) collective-permute-start(bf16[128,8192]{1,0:T(8,128)(2,1)} %get-tuple-element.491), channel_id=1, source_target_pairs={{1,0},{2,1},{3,2},{4,3},{5,4},{6,5},{7,6},{8,7},{9,8},{10,9},{11,1... | collective-permute-start | bytes 6291464 | tf_op jit(solution)/shard_map/while/body/eval_jaxpr/ppermute | solution.py:13
  422.1 27.6 %collective-permute-start = (bf16[128,8192]{1,0:T(8,128)(2,1)}, bf16[128,8192]{1,0:T(8,128)(2,1)S(1)}, u32[]{:S(2)}, u32[]{:S(2)}) collective-permute-start(bf16[128,8192]{1,0:T(8,128)(2,1)} %get-tuple-element.491), channel_id=1, source_target_pairs={{1,0},{2,1},{3,2},{4,3},{5,4},{6,5},{7,6},{8,7},{9,8},{10,9},{11,1... | collective-permute-start | bytes 6291464 | tf_op jit(solution)/shard_map/while/body/eval_jaxpr/ppermute | solution.py:13
  451.2 183.3 %collective-permute-start = (bf16[128,8192]{1,0:T(8,128)(2,1)}, bf16[128,8192]{1,0:T(8,128)(2,1)S(1)}, u32[]{:S(2)}, u32[]{:S(2)}) collective-permute-start(bf16[128,8192]{1,0:T(8,128)(2,1)} %get-tuple-element.491), channel_id=1, source_target_pairs={{1,0},{2,1},{3,2},{4,3},{5,4},{6,5},{7,6},{8,7},{9,8},{10,9},{11,1... | collective-permute-start | bytes 6291464 | tf_op jit(solution)/shard_map/while/body/eval_jaxpr/ppermute | solution.py:13
  634.5 9.0 %slice-start = ((s8[8388608]{0:T(1024)(128)(4,1)}), s8[4194304]{0:T(1024)(128)(4,1)S(1)}, s32[]{:S(2)}) async-start(s8[8388608]{0:T(1024)(128)(4,1)} %bitcast.45), calls=%async_computation | async-start | bytes 8388608 | tf_op jit(solution)/shard_map/while/body/eval_jaxpr/cond
  637.0 6.5 slice-start.1
  656.6 31.2 %collective-permute-start = (bf16[128,8192]{1,0:T(8,128)(2,1)}, bf16[128,8192]{1,0:T(8,128)(2,1)S(1)}, u32[]{:S(2)}, u32[]{:S(2)}) collective-permute-start(bf16[128,8192]{1,0:T(8,128)(2,1)} %get-tuple-element.491), channel_id=1, source_target_pairs={{1,0},{2,1},{3,2},{4,3},{5,4},{6,5},{7,6},{8,7},{9,8},{10,9},{11,1... | collective-permute-start | bytes 6291464 | tf_op jit(solution)/shard_map/while/body/eval_jaxpr/ppermute | solution.py:13
  687.8 9.0 %slice-start = ((s8[8388608]{0:T(1024)(128)(4,1)}), s8[4194304]{0:T(1024)(128)(4,1)S(1)}, s32[]{:S(2)}) async-start(s8[8388608]{0:T(1024)(128)(4,1)} %bitcast.45), calls=%async_computation | async-start | bytes 8388608 | tf_op jit(solution)/shard_map/while/body/eval_jaxpr/cond
  690.3 6.5 slice-start.1
  709.8 31.2 %collective-permute-start = (bf16[128,8192]{1,0:T(8,128)(2,1)}, bf16[128,8192]{1,0:T(8,128)(2,1)S(1)}, u32[]{:S(2)}, u32[]{:S(2)}) collective-permute-start(bf16[128,8192]{1,0:T(8,128)(2,1)} %get-tuple-element.491), channel_id=1, source_target_pairs={{1,0},{2,1},{3,2},{4,3},{5,4},{6,5},{7,6},{8,7},{9,8},{10,9},{11,1... | collective-permute-start | bytes 6291464 | tf_op jit(solution)/shard_map/while/body/eval_jaxpr/ppermute | solution.py:13
  741.0 9.0 %slice-start = ((s8[8388608]{0:T(1024)(128)(4,1)}), s8[4194304]{0:T(1024)(128)(4,1)S(1)}, s32[]{:S(2)}) async-start(s8[8388608]{0:T(1024)(128)(4,1)} %bitcast.45), calls=%async_computation | async-start | bytes 8388608 | tf_op jit(solution)/shard_map/while/body/eval_jaxpr/cond
  743.6 6.5 slice-start.1
  763.1 30.4 %collective-permute-start = (bf16[128,8192]{1,0:T(8,128)(2,1)}, bf16[128,8192]{1,0:T(8,128)(2,1)S(1)}, u32[]{:S(2)}, u32[]{:S(2)}) collective-permute-start(bf16[128,8192]{1,0:T(8,128)(2,1)} %get-tuple-element.491), channel_id=1, source_target_pairs={{1,0},{2,1},{3,2},{4,3},{5,4},{6,5},{7,6},{8,7},{9,8},{10,9},{11,1... | collective-permute-start | bytes 6291464 | tf_op jit(solution)/shard_map/while/body/eval_jaxpr/ppermute | solution.py:13
  793.5 9.0 %slice-start = ((s8[8388608]{0:T(1024)(128)(4,1)}), s8[4194304]{0:T(1024)(128)(4,1)S(1)}, s32[]{:S(2)}) async-start(s8[8388608]{0:T(1024)(128)(4,1)} %bitcast.45), calls=%async_computation | async-start | bytes 8388608 | tf_op jit(solution)/shard_map/while/body/eval_jaxpr/cond
  796.0 6.5 slice-start.1
  815.4 7.2 collective-permute-start
